TPU v7x, 32 devices: a whole 2x2x4 slice. The times are simulated.
32 devices in a mesh: fsdp: 8 (over z, x), rep: 4 (over y, core).
Axes of the slice: x: 2, y: 2, z: 4, core: 2. Of those that a mesh axis runs over, the one named last changes fastest.
Arguments:
- tokens_x: bfloat16 [4096, 8192], P(('fsdp', 'rep')), may hold values from -6 to 6
- cotangent: bfloat16 [4096, 128], P(('fsdp', 'rep')), may hold values from -1 to 1
- master_weight: float32 [8192, 128], P('fsdp'), may hold values from -0.015625 to 0.015625
- first_moment: float32 [8192, 128], P('fsdp'), may hold values from -6 to 6
- second_moment: float32 [8192, 128], P('fsdp'), may hold values from 0.5 to 2
- hidden_dec: bfloat16 [2, 64, 8192], P(None, ('fsdp', 'rep')), may hold values from -6 to 6
- queries: bfloat16 [2, 64, 1024], P(None, ('fsdp', 'rep')), may hold values from -64 to 64
- new_values: bfloat16 [2, 64, 128], P(None, ('fsdp', 'rep')), may hold values from -6 to 6
- key_cache: bfloat16 [64, 1024, 128], P(('fsdp', 'rep')), may hold values from -64 to 64
- value_cache: bfloat16 [64, 1024, 128], P(('fsdp', 'rep')), may hold values from -6 to 6
- cache_lengths: int32 [64], P(('fsdp', 'rep')), may hold values from 2 to 1022, as said below
Outputs:
- weight_next: float32 [8192, 128], P('fsdp')
- first_next: float32 [8192, 128], P('fsdp')
- second_next: float32 [8192, 128], P('fsdp')
- rollout_weight: bfloat16 [8192, 128], replicated
- fresh_keys: bfloat16 [2, 64, 128], P(None, ('fsdp', 'rep'))
- attended: bfloat16 [2, 64, 1024], P(None, ('fsdp', 'rep'))
Inputs may be any that keep to these rules, and one draw needn't show every extreme that they name: `cache_lengths`: some row has exactly 1022 filled slots.
All inputs are finite; a program needn't handle non-finite values. Where the computation divides by a largest or mean magnitude, that divisor is 1e-20 or more.
Results may differ from a plain program's by a relative error of at most 0.0049.
Values may be sent and summed in bfloat16 or wider, within the bound.
A program may use at most 64 MiB of HBM per device.

v0:
```python
import math
import jax
import jax.numpy as jnp
from jax import lax
from jax.sharding import PartitionSpec as P

D = 8192
BLOCK = 128
beta_one = 0.9
beta_two = 0.95
adam_eps = 1e-08
learn_rate = 0.0003
weight_decay = 0.1
step_count = 100
rope_theta = 1000000.0
peak_eps = 1e-06


def adamw(weight, first, second, gradient):
    first_new = beta_one * first + (1.0 - beta_one) * gradient
    second_new = beta_two * second + (1.0 - beta_two) * gradient * gradient
    first_hat = first_new / (1.0 - beta_one**step_count)
    second_hat = second_new / (1.0 - beta_two**step_count)
    weight_new = weight - learn_rate * (
        first_hat / (jnp.sqrt(second_hat) + adam_eps) + weight_decay * weight
    )
    return (weight_new, first_new, second_new)


def rotate(values, positions):
    half = values.shape[-1] // 2
    freq = rope_theta ** (-jnp.arange(half, dtype=jnp.float32) * 2.0 / values.shape[-1])
    angle = positions.astype(jnp.float32)[..., None] * freq
    cosine = jnp.cos(angle)
    sine = jnp.sin(angle)
    first_half = values[..., :half]
    second_half = values[..., half:]
    return jnp.concatenate(
        [first_half * cosine - second_half * sine, second_half * cosine + first_half * sine],
        axis=-1,
    )


def project_keys(hidden_size, quantized_weight, scales, lengths):
    decode_step_count, row_count, block_width = hidden_size.shape
    block_count = scales.shape[0]
    part_count = jnp.einsum(
        "qht,hti->qhi",
        hidden_size.reshape(decode_step_count * row_count, block_count, block_width // block_count),
        quantized_weight.reshape(block_count, block_width // block_count, -1),
        preferred_element_type=jnp.float32,
    )
    raw = jnp.sum(part_count * scales[None, :, None], axis=1).reshape(
        decode_step_count, row_count, -1
    )
    positions = lengths[None, :] + jnp.arange(decode_step_count, dtype=jnp.int32)[:, None]
    return rotate(raw, positions).astype(jnp.bfloat16)


def attend(query, cache_keys, cache_values, fresh, fresh_values, lengths):
    decode_step_count, row_count, joined = query.shape
    head_dim = cache_keys.shape[-1]
    heads = joined // head_dim
    valid = jnp.arange(cache_keys.shape[1], dtype=jnp.int32)[None, None, :] < lengths[:, None, None]
    outputs = []
    for section_index in range(decode_step_count):
        query_now = query[section_index].reshape(row_count, heads, head_dim)
        scores_c = jnp.einsum(
            "rhd,rcd->rhc", query_now, cache_keys, preferred_element_type=jnp.float32
        ) / math.sqrt(head_dim)
        scores_f = jnp.einsum(
            "rhd,trd->rht", query_now, fresh, preferred_element_type=jnp.float32
        ) / math.sqrt(head_dim)
        scores_c = jnp.where(valid, scores_c, -jnp.inf)
        scores_f = jnp.where(
            (jnp.arange(decode_step_count) <= section_index)[None, None, :], scores_f, -jnp.inf
        )
        peak = jnp.maximum(jnp.max(scores_c, axis=2), jnp.max(scores_f, axis=2))[:, :, None]
        exp_c = jnp.exp(scores_c - peak)
        exp_f = jnp.exp(scores_f - peak)
        total = jnp.sum(exp_c, axis=2, keepdims=True) + jnp.sum(exp_f, axis=2, keepdims=True)
        prob_c = (exp_c / total).astype(jnp.bfloat16)
        prob_f = (exp_f / total).astype(jnp.bfloat16)
        mixed = jnp.einsum("rhc,rcd->rhd", prob_c, cache_values, preferred_element_type=jnp.float32)
        mixed = mixed + jnp.einsum(
            "rht,trd->rhd", prob_f, fresh_values, preferred_element_type=jnp.float32
        )
        outputs.append(mixed.reshape(row_count, joined).astype(jnp.bfloat16))
    return jnp.stack(outputs)


def shards(
    tokens_x,
    cotangent,
    master_weight,
    first_moment,
    second_moment,
    hidden_dec,
    queries,
    new_values,
    key_cache,
    value_cache,
    cache_lengths,
):
    shard_rows = master_weight.shape[0]
    partial_grad = lax.psum_scatter(
        lax.dot_general(
            tokens_x, cotangent, (((0,), (0,)), ((), ())), preferred_element_type=jnp.float32
        ),
        "fsdp",
        scatter_dimension=0,
        tiled=True,
    )
    gradient = lax.psum(partial_grad, "rep")
    weight_next, first_next, second_next = adamw(
        master_weight, first_moment, second_moment, gradient
    )
    block_count = D // BLOCK
    row_ids = lax.axis_index("fsdp") * shard_rows + jnp.arange(shard_rows, dtype=jnp.int32)
    member = (row_ids // BLOCK)[:, None] == jnp.arange(block_count, dtype=jnp.int32)[None, :]
    row_peak = jnp.max(jnp.abs(weight_next), axis=1)
    local_peaks = jnp.max(jnp.where(member, row_peak[:, None], 0.0), axis=0)
    scales = lax.pmax(local_peaks, "fsdp") + peak_eps
    row_scale = jnp.sum(jnp.where(member, scales[None, :], 0.0), axis=1)
    local_quant = (weight_next / row_scale[:, None]).astype(jnp.bfloat16)
    rollout_weight = lax.all_gather(local_quant, "fsdp", axis=0, tiled=True)
    fresh_keys = project_keys(hidden_dec, rollout_weight, scales, cache_lengths)
    attended = attend(queries, key_cache, value_cache, fresh_keys, new_values, cache_lengths)
    return (weight_next, first_next, second_next, rollout_weight, fresh_keys, attended)


def solution(mesh):
    return jax.shard_map(
        shards,
        mesh=mesh,
        in_specs=(
            P(("fsdp", "rep"), None),
            P(("fsdp", "rep"), None),
            P("fsdp", None),
            P("fsdp", None),
            P("fsdp", None),
            P(None, ("fsdp", "rep"), None),
            P(None, ("fsdp", "rep"), None),
            P(None, ("fsdp", "rep"), None),
            P(("fsdp", "rep"), None, None),
            P(("fsdp", "rep"), None, None),
            P(("fsdp", "rep")),
        ),
        out_specs=(
            P("fsdp", None),
            P("fsdp", None),
            P("fsdp", None),
            P(),
            P(None, ("fsdp", "rep"), None),
            P(None, ("fsdp", "rep"), None),
        ),
        check_vma=False,
    )
```

profile of v0, /device:TPU:0, one launch (start us, length us, event | category | flops | bytes accessed | tf_op | source)
XLA Modules:
  0.0 224.9 jit_solution(2394929650028422589)
XLA Ops:
  7.2 0.0 copy-start
  7.2 0.0 reduce-scatter.2.cloned.1.call-start
  7.2 1.5 copy-done
  8.8 3.4 %fusion.52 = f32[8192,128]{1,0:T(8,128)} fusion(bf16[128,8192]{1,0:T(8,128)(2,1)S(1)} %copy-done, bf16[128,128]{1,0:T(8,128)(2,1)} %param.12), kind=kOutput, calls=%fused_computation.92 | convolution fusion | flops 268435456 | bytes 6324224 | tf_op jit(solution)/shard_map/dot_general | solution.py:107
  12.2 0.0 reduce-scatter.2.cloned.1.call-update
  12.2 0.0 all-reduce.2.cloned.1.call-start
  12.3 91.1 %reduce-scatter.2.cloned.1.call-done = f32[1024,128]{1,0:T(8,128)} async-done(((f32[8192,128]{1,0:T(8,128)}), f32[1024,128]{1,0:T(8,128)}) %reduce-scatter.2.cloned.1.call-update) | async-done | bytes 524304 | tf_op jit(solution)/shard_map/reduce_scatter | solution.py:106
  103.4 0.0 all-reduce.2.cloned.1.call-update
  103.4 0.0 all-gather.2.cloned.1.call-start
  103.5 0.0 copy-start.4
  103.5 0.0 copy-start.6
  103.5 0.0 copy-start.5
  103.5 0.0 copy-start.1
  103.6 35.3 %all-reduce.2.cloned.1.call-done = f32[1024,128]{1,0:T(8,128)} async-done(((f32[1024,128]{1,0:T(8,128)}), f32[1024,128]{1,0:T(8,128)}) %all-reduce.2.cloned.1.call-update) | async-done | bytes 524304 | tf_op jit(solution)/shard_map/psum | solution.py:114
  138.8 2.9 %abs_reduce_fusion = (f32[1024]{0:T(1024)S(1)}, f32[1024,128]{1,0:T(8,128)S(1)}, f32[1024,128]{1,0:T(8,128)}, f32[1024,128]{1,0:T(8,128)}) fusion(f32[1024,128]{1,0:T(8,128)} %param.13, f32[1024,128]{1,0:T(8,128)} %all-reduce.2.cloned.1.call-done, f32[1024,128]{1,0:T(8,128)} %param.14, f32[1024,128]{1,0:T(8,128)} %param.15), kind=kLoop, calls=%fused_computation.19 | loop fusion | flops 2227200 | bytes 3674112 | tf_op jit(solution)/shard_map/reduce_max | solution.py:121
  141.7 0.0 copy-start.3
  141.7 0.1 select_reduce_fusion.1
  141.9 21.3 %pmax.7 = f32[64]{0:T(128)S(1)} all-reduce(f32[64]{0:T(128)S(1)} %select_reduce_fusion.1), channel_id=1, replica_groups=mesh['fsdp'=8,'rep'=4] {'fsdp'}, use_global_device_ids=true, to_apply=%region_4.5 | all-reduce | flops 64 | bytes 512 | tf_op jit(solution)/shard_map/pmax | solution.py:123
  163.2 0.1 select_reduce_fusion
  163.3 0.0 copy-done.3
  163.3 0.9 divide_convert_fusion
  164.3 0.0 copy-start.2
  164.3 0.0 all-gather.2.cloned.1.call-update
  164.3 0.0 copy-done.4
  164.3 0.1 reshape.145
  164.4 0.0 copy-done.6
  164.4 0.1 add_convert_fusion
  164.5 0.1 iota_compare_fusion.1
  164.6 0.0 copy-done.5
  164.6 0.0 copy-done.1
  164.6 0.0 copy-start.7
  164.6 0.3 fusion.50
  164.9 0.3 fusion.48
  165.3 44.7 %all-gather.2.cloned.1.call-done = bf16[8192,128]{1,0:T(8,128)(2,1)} async-done(((bf16[1024,128]{1,0:T(8,128)(2,1)}), bf16[8192,128]{1,0:T(8,128)(2,1)}) %all-gather.2.cloned.1.call-update) | async-done | bytes 2097168 | tf_op jit(solution)/shard_map/all_gather | solution.py:126
  210.0 2.2 fusion
  212.2 0.1 fusion.47
  212.3 0.1 fusion.37
  212.4 0.1 pad_maximum_fusion.1
  212.5 0.6 copy.32
  213.1 0.1 fusion.49
  213.2 0.1 fusion.51
  213.4 0.2 fusion.12
  213.5 0.0 copy-done.2
  213.5 0.2 fusion.14
  213.8 0.0 copy-done.7
  213.8 0.2 fusion.4
  214.0 0.2 fusion.11
  214.2 0.2 fusion.13
  214.5 0.2 fusion.3
  214.7 0.6 pad_maximum_fusion
  215.3 3.0 %copy.73 = bf16[8192,128]{1,0:T(8,128)(2,1)} copy(bf16[8192,128]{1,0:T(8,128)(2,1)} %all-gather.2.cloned.1.call-done) | data formatting | bytes 4194304
  (14 shorter events, 0.1 us)
Async XLA Ops:
  7.2 1.6 copy-start
  7.2 96.2 %reduce-scatter.2.cloned.1.call-start = ((), (), s32[]{:S(2)}) async-start(), calls=%async_computation.1 | async-start | bytes 4718592 | tf_op jit(solution)/shard_map/reduce_scatter | solution.py:106
  12.2 126.6 %all-reduce.2.cloned.1.call-start = ((), (), s32[]{:S(2)}) async-start(), calls=%async_computation.2 | async-start | bytes 1048576 | tf_op jit(solution)/shard_map/psum | solution.py:114
  103.4 106.5 %all-gather.2.cloned.1.call-start = ((), (), s32[]{:S(2)}) async-start(), calls=%async_computation.3 | async-start | bytes 2359296 | tf_op jit(solution)/shard_map/all_gather | solution.py:126
  103.5 60.8 %copy-start.4 = (bf16[2,2,8192]{2,1,0:T(2,128)(2,1)S(1)}, bf16[2,2,8192]{2,1,0:T(2,128)(2,1)}, u32[]{:S(2)}) copy-start(bf16[2,2,8192]{2,1,0:T(2,128)(2,1)} %param.16) | copy-start | bytes 196612
  103.5 60.9 %copy-start.6 = (s32[2]{0:T(128)S(1)}, s32[2]{0:T(128)}, u32[]{:S(2)}) copy-start(s32[2]{0:T(128)} %param.21) | copy-start | bytes 28
  103.5 61.0 %copy-start.5 = (bf16[2,2,1024]{2,1,0:T(2,128)(2,1)S(1)}, bf16[2,2,1024]{2,1,0:T(2,128)(2,1)}, u32[]{:S(2)}) copy-start(bf16[2,2,1024]{2,1,0:T(2,128)(2,1)} %param.17) | copy-start | bytes 24580
  103.5 61.0 %copy-start.1 = (bf16[2,1024,128]{2,1,0:T(8,128)(2,1)S(1)}, bf16[2,1024,128]{2,1,0:T(8,128)(2,1)}, u32[]{:S(2)}) copy-start(bf16[2,1024,128]{2,1,0:T(8,128)(2,1)} %param.19) | copy-start | bytes 1572868
  141.7 21.6 %copy-start.3 = (f32[1024,128]{1,0:T(8,128)}, f32[1024,128]{1,0:T(8,128)S(1)}, u32[]{:S(2)}) copy-start(f32[1024,128]{1,0:T(8,128)S(1)} %get-tuple-element.48) | copy-start | bytes 1572868
  164.3 49.3 %copy-start.2 = (bf16[2,1024,128]{2,1,0:T(8,128)(2,1)S(1)}, bf16[2,1024,128]{2,1,0:T(8,128)(2,1)}, u32[]{:S(2)}) copy-start(bf16[2,1024,128]{2,1,0:T(8,128)(2,1)} %param.20) | copy-start | bytes 1572868
  164.6 49.2 %copy-start.7 = (bf16[2,2,128]{2,1,0:T(2,128)(2,1)S(1)}, bf16[2,2,128]{2,1,0:T(2,128)(2,1)}, u32[]{:S(2)}) copy-start(bf16[2,2,128]{2,1,0:T(2,128)(2,1)} %param.18) | copy-start | bytes 3076
Sparse Core Ops, SparseCore 0:
  12.3 91.0 reduce-scatter.1
  105.8 33.0 all-reduce.1
  164.4 45.5 all-gather.1
where the time goes:
time: 225 us
  waiting for transfers between devices  171 us (76%)
  blocking collectives  21.3 us (9%)
  between operations  13.9 us (6%)
  matrix products  7.48 us (3%)
  other arithmetic  5.48 us (2%)
  local copies, waits for them, and re-layouts  5.36 us (2%)
    reduce_scatter x1, waiting for transfers between devices, shards(): lax.psum_scatter(lax.dot_general(tokens_x, cotangent, (((0,), (0,)), ((),...  91.1 us
    all_gather x1, waiting for transfers between devices, shards(): rollout_weight = lax.all_gather(local_quant, 'fsdp', axis=0, tiled=True)  44.7 us
    psum x1, waiting for transfers between devices, shards(): gradient = lax.psum(partial_grad, 'rep')  35.3 us
    pmax x1, blocking collectives, shards(): scales = lax.pmax(local_peaks, 'fsdp') + peak_eps  21.3 us
    unnamed x19, local copies, waits for them, and re-layouts  5.2 us
  transfers between devices with their start and end apart: 3, of which 3 were waited for; matrix products, arithmetic and copies ran while one was open for 0% of the time, Pallas kernels for 0%

commit v1 on v0

--- a/solution.py
+++ b/solution.py
@@ -14,6 +14,15 @@
 step_count = 100
 rope_theta = 1000000.0
 peak_eps = 1e-06
+
+
+def doubling_sum(value, axis):
+    size = lax.axis_size(axis)
+    total, hop = (value, 1)
+    while hop < size:
+        total = total + lax.ppermute(total, axis, [(i, i ^ hop) for i in range(size)])
+        hop = 2 * hop
+    return total
 
 
 def adamw(weight, first, second, gradient):
@@ -111,7 +120,7 @@
         scatter_dimension=0,
         tiled=True,
     )
-    gradient = lax.psum(partial_grad, "rep")
+    gradient = doubling_sum(partial_grad, "rep")
     weight_next, first_next, second_next = adamw(
         master_weight, first_moment, second_moment, gradient
     )

time: 225 us -> 207 us (0.920)
  waiting for transfers between devices: 171 us -> 149 us
    psum x1 -> x0, waiting for transfers between devices: 35.3 us -> none  [shards(): gradient = lax.psum(partial_grad, 'rep')]
    ppermute x0 -> x2, waiting for transfers between devices: none -> 14.7 us  [doubling_sum(): lax.ppermute(total, axis, [(i, i ^ hop) for i in range(size)])]
    unnamed x19 -> x17, local copies, waits for them, and re-layouts: 5.2 us -> 5.2 us
  transfers between devices with their start and end apart: 3 -> 4, of which waited for: 3 -> 4; matrix products, arithmetic and copies ran while one was open for 0% -> 1% of each run, Pallas kernels for 0% -> 0%
where the time goes in v1:
time: 207 us
  waiting for transfers between devices  149 us (72%)
  blocking collectives  20 us (10%)
  between operations  14.2 us (7%)
  matrix products  9.57 us (5%)
  other arithmetic  6.62 us (3%)
  local copies, waits for them, and re-layouts  5.36 us (3%)
    reduce_scatter x1, waiting for transfers between devices, shards(): lax.psum_scatter(lax.dot_general(tokens_x, cotangent, (((0,), (0,)), ((),...  91.1 us
    all_gather x1, waiting for transfers between devices, shards(): rollout_weight = lax.all_gather(local_quant, 'fsdp', axis=0, tiled=True)  43.5 us
    pmax x1, blocking collectives, shards(): scales = lax.pmax(local_peaks, 'fsdp') + peak_eps  20 us
    ppermute x2, waiting for transfers between devices, doubling_sum(): lax.ppermute(total, axis, [(i, i ^ hop) for i in range(size)])  14.7 us
    unnamed x17, local copies, waits for them, and re-layouts  5.2 us
  transfers between devices with their start and end apart: 4, of which 4 were waited for; matrix products, arithmetic and copies ran while one was open for 1% of the time, Pallas kernels for 0%

profile of v1, /device:TPU:0, one launch (start us, length us, event | category | flops | bytes accessed | tf_op | source)
XLA Modules:
  0.0 206.7 jit_solution(8100989633884629714)
XLA Ops:
  7.2 0.0 copy-start
  7.2 0.0 reduce-scatter.2.cloned.1.call-start
  7.2 1.5 copy-done
  8.8 3.4 %fusion.52 = f32[8192,128]{1,0:T(8,128)} fusion(bf16[128,8192]{1,0:T(8,128)(2,1)S(1)} %copy-done, bf16[128,128]{1,0:T(8,128)(2,1)} %param.12), kind=kOutput, calls=%fused_computation.92 | convolution fusion | flops 268435456 | bytes 6324224 | tf_op jit(solution)/shard_map/dot_general | solution.py:116
  12.2 0.0 reduce-scatter.2.cloned.1.call-update
  12.2 0.0 all-gather.2.cloned.1.call-start
  12.3 91.1 %reduce-scatter.2.cloned.1.call-done = f32[1024,128]{1,0:T(8,128)} async-done(((f32[8192,128]{1,0:T(8,128)}), f32[1024,128]{1,0:T(8,128)}) %reduce-scatter.2.cloned.1.call-update) | async-done | bytes 524304 | tf_op jit(solution)/shard_map/reduce_scatter | solution.py:115
  103.4 0.0 collective-permute-start
  103.4 2.1 %collective-permute-done = f32[1024,128]{1,0:T(8,128)S(1)} collective-permute-done((f32[1024,128]{1,0:T(8,128)}, f32[1024,128]{1,0:T(8,128)S(1)}, u32[]{:S(2)}, u32[]{:S(2)}) %collective-permute-start) | collective-permute-done | bytes 524320 | tf_op jit(solution)/shard_map/ppermute | solution.py:23
  105.5 1.1 add.86
  106.7 1.5 collective-permute-start.1
  108.2 0.0 copy-start.3
  108.2 0.0 copy-start.5
  108.2 0.0 copy-start.4
  108.2 12.6 %collective-permute-done.1 = f32[1024,128]{1,0:T(8,128)} collective-permute-done((f32[1024,128]{1,0:T(8,128)S(1)}, f32[1024,128]{1,0:T(8,128)}, u32[]{:S(2)}, u32[]{:S(2)}) %collective-permute-start.1) | collective-permute-done | bytes 524320 | tf_op jit(solution)/shard_map/ppermute | solution.py:23
  120.8 2.9 %abs_reduce_fusion = (f32[1024]{0:T(1024)S(1)}, f32[1024,128]{1,0:T(8,128)S(1)}, f32[1024,128]{1,0:T(8,128)}, f32[1024,128]{1,0:T(8,128)}) fusion(f32[1024,128]{1,0:T(8,128)} %param.13, f32[1024,128]{1,0:T(8,128)S(1)} %add.86, f32[1024,128]{1,0:T(8,128)} %collective-permute-done.1, f32[1024,128]{1,0:T(8,128)} %param.14, f32[1024,128]{1,0:T(8,128)} %param.15), kind=kLoop, calls=%fused_computation.19 | loop fusion | flops 2358272 | bytes 4198400 | tf_op jit(solution)/shard_map/reduce_max | solution.py:130
  123.7 0.0 copy-start.1
  123.7 0.1 select_reduce_fusion.1
  123.8 20.0 %pmax.7 = f32[64]{0:T(128)S(1)} all-reduce(f32[64]{0:T(128)S(1)} %select_reduce_fusion.1), channel_id=1, replica_groups=mesh['fsdp'=8,'rep'=4] {'fsdp'}, use_global_device_ids=true, to_apply=%region_3.4 | all-reduce | flops 64 | bytes 512 | tf_op jit(solution)/shard_map/pmax | solution.py:132
  143.9 0.1 select_reduce_fusion
  144.0 0.9 divide_convert_fusion
  144.9 0.0 copy-start.2
  144.9 0.0 all-gather.2.cloned.1.call-update
  144.9 0.0 copy-done.3
  144.9 0.1 reshape.145
  145.0 0.0 copy-done.5
  145.1 0.1 add_convert_fusion
  145.1 0.1 iota_compare_fusion.1
  145.2 0.0 copy-done.4
  145.2 0.0 copy-start.6
  145.2 1.4 fusion.50
  146.6 1.4 fusion.48
  148.0 43.5 %all-gather.2.cloned.1.call-done = bf16[8192,128]{1,0:T(8,128)(2,1)} async-done(((bf16[1024,128]{1,0:T(8,128)(2,1)}), bf16[8192,128]{1,0:T(8,128)(2,1)}) %all-gather.2.cloned.1.call-update) | async-done | bytes 2097168 | tf_op jit(solution)/shard_map/all_gather | solution.py:135
  191.4 2.2 %fusion = f32[128,4]{0,1:T(4,128)S(1)} fusion(bf16[64,128,128]{2,1,0:T(8,128)(2,1)} %bitcast.41, bf16[4,64,128]{2,1,0:T(8,128)(2,1)S(1)} %reshape.145, f32[64]{0:T(128)S(1)} %broadcast_add_fusion), kind=kOutput, calls=%fused_computation.1 | convolution fusion | flops 8453632 | bytes 2164992 | tf_op jit(solution)/shard_map/qht,hti->qhi/dot_general | solution.py:56
  193.7 0.0 copy-done.1
  193.7 0.1 fusion.47
  193.8 0.1 fusion.37
  193.9 0.1 pad_maximum_fusion.1
  194.0 0.6 copy.32
  194.5 0.1 fusion.49
  194.7 0.1 fusion.51
  194.8 0.2 fusion.12
  195.0 0.0 copy-done.2
  195.0 0.2 fusion.14
  195.3 0.0 copy-done.6
  195.3 0.2 fusion.4
  195.5 0.2 fusion.11
  195.7 0.2 fusion.13
  195.9 0.2 fusion.3
  196.2 0.6 pad_maximum_fusion
  196.8 3.0 %copy.72 = bf16[8192,128]{1,0:T(8,128)(2,1)} copy(bf16[8192,128]{1,0:T(8,128)(2,1)} %all-gather.2.cloned.1.call-done) | data formatting | bytes 4194304
  (14 shorter events, 0.1 us)
Async XLA Ops:
  7.2 1.6 copy-start
  7.2 96.2 %reduce-scatter.2.cloned.1.call-start = ((), (), s32[]{:S(2)}) async-start(), calls=%async_computation.1 | async-start | bytes 4718592 | tf_op jit(solution)/shard_map/reduce_scatter | solution.py:115
  12.2 179.2 %all-gather.2.cloned.1.call-start = ((), (), s32[]{:S(2)}) async-start(), calls=%async_computation.2 | async-start | bytes 2359296 | tf_op jit(solution)/shard_map/all_gather | solution.py:135
  103.4 2.1 %collective-permute-start = (f32[1024,128]{1,0:T(8,128)}, f32[1024,128]{1,0:T(8,128)S(1)}, u32[]{:S(2)}, u32[]{:S(2)}) collective-permute-start(f32[1024,128]{1,0:T(8,128)} %reduce-scatter.2.cloned.1.call-done), channel_id=1, source_target_pairs={{0,1},{1,0},{2,3},{3,2},{4,5},{5,4},{6,7},{7,6},{8,9},{9,8},{10,11... | collective-permute-start | bytes 1572872 | tf_op jit(solution)/shard_map/ppermute | solution.py:23
  106.7 14.1 %collective-permute-start.1 = (f32[1024,128]{1,0:T(8,128)S(1)}, f32[1024,128]{1,0:T(8,128)}, u32[]{:S(2)}, u32[]{:S(2)}) collective-permute-start(f32[1024,128]{1,0:T(8,128)S(1)} %add.86), channel_id=1, source_target_pairs={{0,2},{1,3},{2,0},{3,1},{4,6},{5,7},{6,4},{7,5},{8,10},{9,11},{10,... | collective-permute-start | bytes 1572872 | tf_op jit(solution)/shard_map/ppermute | solution.py:23
  108.2 36.7 %copy-start.3 = (bf16[2,2,8192]{2,1,0:T(2,128)(2,1)S(1)}, bf16[2,2,8192]{2,1,0:T(2,128)(2,1)}, u32[]{:S(2)}) copy-start(bf16[2,2,8192]{2,1,0:T(2,128)(2,1)} %param.16) | copy-start | bytes 196612
  108.2 36.8 %copy-start.5 = (s32[2]{0:T(128)S(1)}, s32[2]{0:T(128)}, u32[]{:S(2)}) copy-start(s32[2]{0:T(128)} %param.21) | copy-start | bytes 28
  108.2 37.0 %copy-start.4 = (bf16[2,2,1024]{2,1,0:T(2,128)(2,1)S(1)}, bf16[2,2,1024]{2,1,0:T(2,128)(2,1)}, u32[]{:S(2)}) copy-start(bf16[2,2,1024]{2,1,0:T(2,128)(2,1)} %param.17) | copy-start | bytes 24580
  123.7 70.0 %copy-start.1 = (f32[1024,128]{1,0:T(8,128)}, f32[1024,128]{1,0:T(8,128)S(1)}, u32[]{:S(2)}) copy-start(f32[1024,128]{1,0:T(8,128)S(1)} %get-tuple-element.48) | copy-start | bytes 1572868
  144.9 50.1 %copy-start.2 = (bf16[2,1024,128]{2,1,0:T(8,128)(2,1)S(1)}, bf16[2,1024,128]{2,1,0:T(8,128)(2,1)}, u32[]{:S(2)}) copy-start(bf16[2,1024,128]{2,1,0:T(8,128)(2,1)} %param.20) | copy-start | bytes 1572868
  145.2 50.0 %copy-start.6 = (bf16[2,2,128]{2,1,0:T(2,128)(2,1)S(1)}, bf16[2,2,128]{2,1,0:T(2,128)(2,1)}, u32[]{:S(2)}) copy-start(bf16[2,2,128]{2,1,0:T(2,128)(2,1)} %param.18) | copy-start | bytes 3076
Sparse Core Ops, SparseCore 0:
  12.3 91.0 reduce-scatter.1
  145.1 46.3 all-gather.1
